TPU v7x, 512 devices: a whole 4x4x16 slice. The times are simulated.
512 devices in a mesh: region: 64 (over z, x), split: 8 (over y, core).
Axes of the slice: x: 4, y: 4, z: 16, core: 2. Of those that a mesh axis runs over, the one named last changes fastest.
Arguments:
- vectors: float32 [294912, 256], P(('region', 'split'))
- hessian: bfloat16 [1536, 12, 192, 192], P(('region', 'split')), may hold values from -0.125 to 0.125
- block_cols: int32 [1536, 12], P(('region', 'split')), may hold values from 0 to 35, as said below
- live_blocks: int32 [1536], P(('region', 'split')), may hold values from 6 to 12, as said below
- halo_lists: int32 [64, 2, 6], P('region'), may hold values from 0 to 23, as said below
- bounds: float32 [2], replicated, as said below
Outputs:
- basis: float32 [294912, 256], P(('region', 'split'))
- projected: float32 [256, 256], replicated
Inputs may be any that keep to these rules, and one draw needn't show every extreme that they name: `block_cols`: in each row the entries are distinct and entry 0 is the row's own block within its region; values below 24 name blocks of the row's region, 24 + j the j-th block received from the lower region, 30 + j the j-th from the upper region. `live_blocks`: the first block row of every region has all 12 blocks intact. `halo_lists`: each list holds distinct block indices within the region. bounds[0] < 0 < bounds[1].
All inputs are finite; a program needn't handle non-finite values.
Results may differ from a plain program's by a relative error of at most 0.0005.
The roundings to bfloat16 on the way count: a program that leaves them out, or rounds other values in their place, can miss the bound.
Values may be sent and summed in bfloat16 or wider, within the bound.
A program may use at most 64 MiB of HBM per device.

v0:
```python
import jax
import jax.numpy as jnp
from jax import lax
from jax.sharding import PartitionSpec as P


def shifted(value, axis, steps):
    count = lax.axis_size(axis)
    pairs = [(source, (source + steps) % count) for source in range(count)]
    return lax.ppermute(value, axis, pairs)


def apply_blocks(operand, hessian, block_cols, live_blocks, halo_lists):
    row_blocks = hessian.shape[0]
    block_size = hessian.shape[2]
    mode_count = operand.shape[1]
    shard_blocks = operand.reshape(row_blocks, block_size, mode_count)
    region = lax.all_gather(shard_blocks, "split", axis=0, tiled=True)
    send_lower = region[halo_lists[0, 0]]
    send_upper = region[halo_lists[0, 1]]
    from_lower = shifted(send_upper, "region", 1)
    from_upper = shifted(send_lower, "region", -1)
    candidates = jnp.concatenate([region, from_lower, from_upper], 0)
    picked = candidates[block_cols]
    used_mask = lax.broadcasted_iota(jnp.int32, block_cols.shape, 1) < live_blocks[:, None]
    picked = jnp.where(used_mask[:, :, None, None], picked, jnp.zeros((), jnp.bfloat16))
    product = jnp.einsum("rkij,rkjm->rim", hessian, picked, preferred_element_type=jnp.float32)
    return product.reshape(row_blocks * block_size, mode_count)


def local(vectors, hessian, block_cols, live_blocks, halo_lists, bounds):
    centre = 0.5 * (bounds[0] + bounds[1])
    half_width = 0.5 * (bounds[1] - bounds[0])
    first = apply_blocks(vectors.astype(jnp.bfloat16), hessian, block_cols, live_blocks, halo_lists)
    filtered_one = (first - centre * vectors) / half_width
    second = apply_blocks(
        filtered_one.astype(jnp.bfloat16), hessian, block_cols, live_blocks, halo_lists
    )
    filtered_two = 2.0 * (second - centre * filtered_one) / half_width - vectors
    image = apply_blocks(
        filtered_two.astype(jnp.bfloat16), hessian, block_cols, live_blocks, halo_lists
    )
    total_rows = vectors.shape[0] * lax.axis_size("region") * lax.axis_size("split")
    contract = (((0,), (0,)), ((), ()))
    gram_part = lax.dot_general(
        filtered_two, filtered_two, contract, precision=lax.Precision.HIGHEST
    )
    cross_part = lax.dot_general(filtered_two, image, contract, precision=lax.Precision.HIGHEST)
    gram, cross = lax.psum((gram_part, cross_part), ("region", "split"))
    gram = gram / total_rows
    cross = cross / total_rows
    lower = jnp.linalg.cholesky(gram)
    basis = jax.scipy.linalg.solve_triangular(lower, filtered_two.T, lower=True).T
    partial_left = jax.scipy.linalg.solve_triangular(lower, cross, lower=True)
    projected = jax.scipy.linalg.solve_triangular(lower, partial_left.T, lower=True).T
    return (basis, projected)


def solution(mesh):
    placed = (
        P(("region", "split"), None),
        P(("region", "split"), None, None, None),
        P(("region", "split"), None),
        P(("region", "split")),
        P("region", None, None),
        P(),
    )
    return jax.shard_map(
        local,
        mesh=mesh,
        in_specs=placed,
        out_specs=(P(("region", "split"), None), P()),
        check_vma=False,
    )
```

profile of v0, /device:TPU:1, one launch (start us, length us, event | category | flops | bytes accessed | tf_op | source)
XLA Modules:
  0.0 814.2 jit_solution(8782221556383976657)
XLA Ops:
  10.1 39.6 %all-gather.4.cloned.1.call-done = bf16[24,192,256]{2,1,0:T(8,128)(2,1)} async-done(((bf16[3,192,256]{2,1,0:T(8,128)(2,1)}), bf16[24,192,256]{2,1,0:T(8,128)(2,1)}) %all-gather.4.cloned.1.call-update) | async-done | bytes 2359312 | tf_op jit(solution)/shard_map/all_gather | solution.py:18
  49.7 3.1 gather_fusion
  52.8 3.1 collective-permute-start
  59.0 6.6 collective-permute-start.1
  69.7 4.6 collective-permute-done
  74.3 4.0 collective-permute-done.1
  78.3 3.4 pad_maximum_fusion
  81.7 4.8 gather_fusion.2
  90.6 34.4 %all-gather.6.cloned.1.call-done = bf16[24,192,256]{2,1,0:T(8,128)(2,1)} async-done(((bf16[3,192,256]{2,1,0:T(8,128)(2,1)}), bf16[24,192,256]{2,1,0:T(8,128)(2,1)}) %all-gather.6.cloned.1.call-update) | async-done | bytes 2359312 | tf_op jit(solution)/shard_map/all_gather | solution.py:18
  125.0 3.1 gather_fusion.3
  128.1 3.1 collective-permute-start.2
  131.2 3.1 gather_fusion.4
  134.3 6.6 collective-permute-start.3
  141.0 8.7 %collective-permute-done.2 = bf16[6,192,256]{2,1,0:T(8,128)(2,1)} collective-permute-done((bf16[6,192,256]{2,1,0:T(8,128)(2,1)}, bf16[6,192,256]{2,1,0:T(8,128)(2,1)}, u32[]{:S(2)}, u32[]{:S(2)}) %collective-permute-start.2) | collective-permute-done | bytes 589856 | tf_op jit(solution)/shard_map/ppermute | solution.py:10
  149.7 4.0 collective-permute-done.3
  153.7 3.3 pad_maximum_fusion.1
  157.0 4.8 gather_fusion.5
  166.1 34.3 %all-gather.8.cloned.1.call-done = bf16[24,192,256]{2,1,0:T(8,128)(2,1)} async-done(((bf16[3,192,256]{2,1,0:T(8,128)(2,1)}), bf16[24,192,256]{2,1,0:T(8,128)(2,1)}) %all-gather.8.cloned.1.call-update) | async-done | bytes 2359312 | tf_op jit(solution)/shard_map/all_gather | solution.py:18
  200.5 3.1 gather_fusion.6
  206.7 3.1 gather_fusion.7
  209.8 6.6 collective-permute-start.5
  216.4 3.2 fusion.42
  219.6 5.5 collective-permute-done.4
  225.1 4.0 collective-permute-done.5
  229.1 3.3 pad_maximum_fusion.2
  232.5 4.8 gather_fusion.8
  242.3 466.4 %all-reduce.4.cloned.1.call-done = (f32[256,256]{0,1:T(8,128)}, f32[256,256]{0,1:T(8,128)}) async-done(((f32[256,256]{0,1:T(8,128)}, f32[256,256]{0,1:T(8,128)}), (f32[256,256]{0,1:T(8,128)}, f32[256,256]{0,1:T(8,128)})) %all-reduce.4.cloned.1.call-update) | async-done | bytes 524304 | tf_op jit(solution)/shard_map/psum | solution.py:49
  714.8 13.2 %cholesky.50 = f32[128,128]{1,0:T(8,128)} custom-call(f32[128,128]{1,0:T(8,128)} %cholesky.118), custom_call_target="Cholesky" | custom-call | tf_op jit(solution)/shard_map/jit(cholesky)/cholesky | solution.py:52
  731.0 11.3 %custom-call.18 = f32[1,128,128]{1,2,0:T(8,128)} custom-call(f32[1,128,128]{2,1,0:T(8,128)} %get-tuple-element.48), custom_call_target="InvertDiagBlocksLowerTriangular" | custom-call | tf_op jit(solution)/shard_map/jit(cholesky)/cholesky | solution.py:52
  745.7 13.4 %cholesky.105 = f32[128,128]{1,0:T(8,128)} custom-call(f32[128,128]{1,0:T(8,128)} %convolution_subtract_fusion.3), custom_call_target="Cholesky" | custom-call | tf_op jit(solution)/shard_map/jit(cholesky)/cholesky | solution.py:52
  765.0 6.9 while.5
  771.8 21.1 %custom-call.19 = f32[2,128,128]{1,2,0:T(8,128)} custom-call(f32[2,128,128]{2,1,0:T(8,128)} %get-tuple-element.18), custom_call_target="InvertDiagBlocksLowerTriangular" | custom-call | tf_op jit(solution)/shard_map/jit(_solve_triangular)/triangular_solve | solution.py:53
  (77 shorter events, 62.4 us)
Async XLA Ops:
  7.2 79.4 %copy-start = (bf16[3,12,192,192]{3,2,1,0:T(8,128)(2,1)S(1)}, bf16[3,12,192,192]{3,2,1,0:T(8,128)(2,1)}, u32[]{:S(2)}) copy-start(bf16[3,12,192,192]{3,2,1,0:T(8,128)(2,1)} %param.9) | copy-start | bytes 7962628
  7.2 58.4 %copy-start.8 = (f32[2]{0:T(128)S(1)}, f32[2]{0:T(128)}, u32[]{:S(2)}) copy-start(f32[2]{0:T(128)} %param.13) | copy-start | bytes 28
  7.2 61.7 %copy-start.7 = (s32[3,12]{1,0:T(4,128)S(1)}, s32[3,12]{1,0:T(4,128)}, u32[]{:S(2)}) copy-start(s32[3,12]{1,0:T(4,128)} %param.10) | copy-start | bytes 436
  7.2 42.5 %all-gather.4.cloned.1.call-start = ((), (), s32[]{:S(2)}) async-start(), calls=%async_computation | async-start | bytes 2654208 | tf_op jit(solution)/shard_map/all_gather | solution.py:18
  9.2 115.8 %all-gather.6.cloned.1.call-start = ((), (), s32[]{:S(2)}) async-start(), calls=%async_computation.1 | async-start | bytes 2654208 | tf_op jit(solution)/shard_map/all_gather | solution.py:18
  52.8 21.5 %collective-permute-start = (bf16[6,192,256]{2,1,0:T(8,128)(2,1)}, bf16[6,192,256]{2,1,0:T(8,128)(2,1)}, u32[]{:S(2)}, u32[]{:S(2)}) collective-permute-start(bf16[6,192,256]{2,1,0:T(8,128)(2,1)} %gather_fusion), channel_id=1, source_target_pairs={{0,8},{8,16},{16,24},{24,32},{32,40},{40,48},{48,56},{56,64},{64,7... | collective-permute-start | bytes 1769480 | tf_op jit(solution)/shard_map/ppermute | solution.py:10
  59.0 19.3 %collective-permute-start.1 = (bf16[6,192,256]{2,1,0:T(8,128)(2,1)}, bf16[6,192,256]{2,1,0:T(8,128)(2,1)}, u32[]{:S(2)}, u32[]{:S(2)}) collective-permute-start(bf16[6,192,256]{2,1,0:T(8,128)(2,1)} %gather_fusion.1), channel_id=1, source_target_pairs={{0,504},{8,0},{16,8},{24,16},{32,24},{40,32},{48,40},{56,48},{64,5... | collective-permute-start | bytes 1769480 | tf_op jit(solution)/shard_map/ppermute | solution.py:10
  86.6 3.1 copy-start.2
  89.6 0.9 copy-start.4
  90.6 109.9 %all-gather.8.cloned.1.call-start = ((), (), s32[]{:S(2)}) async-start(), calls=%async_computation.2 | async-start | bytes 2654208 | tf_op jit(solution)/shard_map/all_gather | solution.py:18
  128.1 21.5 %collective-permute-start.2 = (bf16[6,192,256]{2,1,0:T(8,128)(2,1)}, bf16[6,192,256]{2,1,0:T(8,128)(2,1)}, u32[]{:S(2)}, u32[]{:S(2)}) collective-permute-start(bf16[6,192,256]{2,1,0:T(8,128)(2,1)} %gather_fusion.3), channel_id=1, source_target_pairs={{0,8},{8,16},{16,24},{24,32},{32,40},{40,48},{48,56},{56,64},{64,7... | collective-permute-start | bytes 1769480 | tf_op jit(solution)/shard_map/ppermute | solution.py:10
  134.3 19.3 %collective-permute-start.3 = (bf16[6,192,256]{2,1,0:T(8,128)(2,1)}, bf16[6,192,256]{2,1,0:T(8,128)(2,1)S(1)}, u32[]{:S(2)}, u32[]{:S(2)}) collective-permute-start(bf16[6,192,256]{2,1,0:T(8,128)(2,1)} %gather_fusion.4), channel_id=1, source_target_pairs={{0,504},{8,0},{16,8},{24,16},{32,24},{40,32},{48,40},{56,48},{64,5... | collective-permute-start | bytes 1769480 | tf_op jit(solution)/shard_map/ppermute | solution.py:10
  161.9 3.1 copy-start.3
  161.9 3.1 copy-start.5
  166.1 542.7 %all-reduce.4.cloned.1.call-start = ((), (), s32[]{:S(2)}) async-start(), calls=%async_computation.3 | async-start | bytes 1048576 | tf_op jit(solution)/shard_map/psum | solution.py:49
  203.6 21.5 %collective-permute-start.4 = (bf16[6,192,256]{2,1,0:T(8,128)(2,1)}, bf16[6,192,256]{2,1,0:T(8,128)(2,1)}, u32[]{:S(2)}, u32[]{:S(2)}) collective-permute-start(bf16[6,192,256]{2,1,0:T(8,128)(2,1)} %gather_fusion.6), channel_id=1, source_target_pairs={{0,8},{8,16},{16,24},{24,32},{32,40},{40,48},{48,56},{56,64},{64,7... | collective-permute-start | bytes 1769480 | tf_op jit(solution)/shard_map/ppermute | solution.py:10
  209.8 19.3 %collective-permute-start.5 = (bf16[6,192,256]{2,1,0:T(8,128)(2,1)}, bf16[6,192,256]{2,1,0:T(8,128)(2,1)S(1)}, u32[]{:S(2)}, u32[]{:S(2)}) collective-permute-start(bf16[6,192,256]{2,1,0:T(8,128)(2,1)} %gather_fusion.7), channel_id=1, source_target_pairs={{0,504},{8,0},{16,8},{24,16},{32,24},{40,32},{48,40},{56,48},{64,5... | collective-permute-start | bytes 1769480 | tf_op jit(solution)/shard_map/ppermute | solution.py:10
  237.3 3.0 copy-start.1
  713.5 0.7 copy-start.6
Sparse Core Ops, SparseCore 0:
  10.7 38.9 all-gather.3
  90.7 34.3 all-gather.5
  166.2 34.2 all-gather.7
  242.4 466.3 all-reduce.3
where the time goes:
time: 816 us; the launch traced here: 814 us
  waiting for transfers between devices  606 us (74%)
  other arithmetic  85.1 us (10%)
  local copies, waits for them, and re-layouts  47.2 us (6%)
  starting transfers between devices  29.3 us (4%)
  matrix products  29 us (4%)
  between operations  18 us (2%)
    psum x1, waiting for transfers between devices, local(): gram, cross = lax.psum((gram_part, cross_part), ('region', 'split'))  466 us
    all_gather x3, waiting for transfers between devices, apply_blocks(): region = lax.all_gather(shard_blocks, 'split', axis=0, tiled=True)  108 us
    another operation x7, other arithmetic, local(): lower = jnp.linalg.cholesky(gram)  42.1 us
    ppermute x6, waiting for transfers between devices, shifted(): return lax.ppermute(value, axis, pairs)  30.8 us
    ppermute x6, starting transfers between devices, shifted(): return lax.ppermute(value, axis, pairs)  29.1 us
    another operation x3, other arithmetic, local(): jax.scipy.linalg.solve_triangular(lower, filtered_two.T, lower=True)  22.8 us
  transfers between devices with their start and end apart: 10, of which 10 were waited for; matrix products, arithmetic and copies ran while one was open for 2% of the time, Pallas kernels for 0%

commit v1 on v0

--- a/solution.py
+++ b/solution.py
@@ -46,7 +46,7 @@
         filtered_two, filtered_two, contract, precision=lax.Precision.HIGHEST
     )
     cross_part = lax.dot_general(filtered_two, image, contract, precision=lax.Precision.HIGHEST)
-    gram, cross = lax.psum((gram_part, cross_part), ("region", "split"))
+    gram, cross = lax.psum(lax.psum((gram_part, cross_part), "region"), "split")
     gram = gram / total_rows
     cross = cross / total_rows
     lower = jnp.linalg.cholesky(gram)

time: 816 us -> 691 us (0.85)
  waiting for transfers between devices: 606 us -> 481 us
    psum x1 -> x2, waiting for transfers between devices: 466 us -> 341 us  [local(): gram, cross = lax.psum(lax.psum((gram_part, cross_part), 'region'), 'split')]
  transfers between devices with their start and end apart: 10 -> 11, of which waited for: 10 -> 11; matrix products, arithmetic and copies ran while one was open for 2% -> 2% of each run, Pallas kernels for 0% -> 0%
where the time goes in v1:
time: 691 us; the launch traced here: 689 us
  waiting for transfers between devices  481 us (70%)
  other arithmetic  84.8 us (12%)
  local copies, waits for them, and re-layouts  47.1 us (7%)
  starting transfers between devices  29.5 us (4%)
  matrix products  29 us (4%)
  between operations  17.8 us (3%)
    psum x2, waiting for transfers between devices, local(): gram, cross = lax.psum(lax.psum((gram_part, cross_part), 'region'), 'split')  341 us
    all_gather x3, waiting for transfers between devices, apply_blocks(): region = lax.all_gather(shard_blocks, 'split', axis=0, tiled=True)  108 us
    another operation x7, other arithmetic, local(): lower = jnp.linalg.cholesky(gram)  42 us
    ppermute x6, waiting for transfers between devices, shifted(): return lax.ppermute(value, axis, pairs)  31.1 us
    ppermute x6, starting transfers between devices, shifted(): return lax.ppermute(value, axis, pairs)  29.1 us
    another operation x3, other arithmetic, local(): jax.scipy.linalg.solve_triangular(lower, filtered_two.T, lower=True)  22.8 us
    gather x3, local copies, waits for them, and re-layouts, apply_blocks(): picked = candidates[block_cols]  14.5 us
  transfers between devices with their start and end apart: 11, of which 11 were waited for; matrix products, arithmetic and copies ran while one was open for 2% of the time, Pallas kernels for 0%

profile of v1, /device:TPU:1, one launch (start us, length us, event | category | flops | bytes accessed | tf_op | source)
XLA Modules:
  0.0 689.1 jit_solution(13045528527895492048)
XLA Ops:
  10.1 39.6 %all-gather.4.cloned.1.call-done = bf16[24,192,256]{2,1,0:T(8,128)(2,1)} async-done(((bf16[3,192,256]{2,1,0:T(8,128)(2,1)}), bf16[24,192,256]{2,1,0:T(8,128)(2,1)}) %all-gather.4.cloned.1.call-update) | async-done | bytes 2359312 | tf_op jit(solution)/shard_map/all_gather | solution.py:18
  49.7 3.1 gather_fusion
  52.8 3.1 collective-permute-start
  59.0 6.6 collective-permute-start.1
  69.5 4.9 collective-permute-done
  74.3 4.0 collective-permute-done.1
  78.3 3.4 pad_maximum_fusion
  81.7 4.8 gather_fusion.2
  90.6 34.4 %all-gather.6.cloned.1.call-done = bf16[24,192,256]{2,1,0:T(8,128)(2,1)} async-done(((bf16[3,192,256]{2,1,0:T(8,128)(2,1)}), bf16[24,192,256]{2,1,0:T(8,128)(2,1)}) %all-gather.6.cloned.1.call-update) | async-done | bytes 2359312 | tf_op jit(solution)/shard_map/all_gather | solution.py:18
  125.0 3.1 gather_fusion.3
  131.2 3.1 gather_fusion.4
  134.3 6.6 collective-permute-start.3
  140.9 8.7 %collective-permute-done.2 = bf16[6,192,256]{2,1,0:T(8,128)(2,1)} collective-permute-done((bf16[6,192,256]{2,1,0:T(8,128)(2,1)}, bf16[6,192,256]{2,1,0:T(8,128)(2,1)}, u32[]{:S(2)}, u32[]{:S(2)}) %collective-permute-start.2) | collective-permute-done | bytes 589856 | tf_op jit(solution)/shard_map/ppermute | solution.py:10
  149.6 4.0 collective-permute-done.3
  153.6 3.3 pad_maximum_fusion.1
  157.0 4.8 gather_fusion.5
  166.1 34.3 %all-gather.8.cloned.1.call-done = bf16[24,192,256]{2,1,0:T(8,128)(2,1)} async-done(((bf16[3,192,256]{2,1,0:T(8,128)(2,1)}), bf16[24,192,256]{2,1,0:T(8,128)(2,1)}) %all-gather.8.cloned.1.call-update) | async-done | bytes 2359312 | tf_op jit(solution)/shard_map/all_gather | solution.py:18
  200.4 3.1 gather_fusion.6
  206.6 3.1 gather_fusion.7
  209.7 6.6 collective-permute-start.5
  216.3 3.2 fusion.42
  219.5 5.5 collective-permute-done.4
  225.0 4.0 collective-permute-done.5
  229.0 3.3 pad_maximum_fusion.2
  232.3 4.8 gather_fusion.8
  242.4 259.7 %all-reduce.6.cloned.1.call-done = (f32[256,256]{0,1:T(8,128)}, f32[256,256]{0,1:T(8,128)}) async-done(((f32[256,256]{0,1:T(8,128)}, f32[256,256]{0,1:T(8,128)}), (f32[256,256]{0,1:T(8,128)}, f32[256,256]{0,1:T(8,128)})) %all-reduce.6.cloned.1.call-update) | async-done | bytes 524304 | tf_op jit(solution)/shard_map/psum | solution.py:49
  502.2 81.7 %all-reduce.8.cloned.1.call-done = (f32[256,256]{0,1:T(8,128)}, f32[256,256]{0,1:T(8,128)}) async-done(((f32[256,256]{0,1:T(8,128)}, f32[256,256]{0,1:T(8,128)}), (f32[256,256]{0,1:T(8,128)}, f32[256,256]{0,1:T(8,128)})) %all-reduce.8.cloned.1.call-update) | async-done | bytes 524304 | tf_op jit(solution)/shard_map/psum | solution.py:49
  589.9 13.2 %cholesky.50 = f32[128,128]{1,0:T(8,128)} custom-call(f32[128,128]{1,0:T(8,128)} %cholesky.118), custom_call_target="Cholesky" | custom-call | tf_op jit(solution)/shard_map/jit(cholesky)/cholesky | solution.py:52
  606.1 11.3 %custom-call.18 = f32[1,128,128]{1,2,0:T(8,128)} custom-call(f32[1,128,128]{2,1,0:T(8,128)} %get-tuple-element.50), custom_call_target="InvertDiagBlocksLowerTriangular" | custom-call | tf_op jit(solution)/shard_map/jit(cholesky)/cholesky | solution.py:52
  620.9 13.2 %cholesky.105 = f32[128,128]{1,0:T(8,128)} custom-call(f32[128,128]{1,0:T(8,128)} %convolution_subtract_fusion.3), custom_call_target="Cholesky" | custom-call | tf_op jit(solution)/shard_map/jit(cholesky)/cholesky | solution.py:52
  639.9 6.8 while.5
  646.7 21.1 %custom-call.19 = f32[2,128,128]{1,2,0:T(8,128)} custom-call(f32[2,128,128]{2,1,0:T(8,128)} %get-tuple-element.18), custom_call_target="InvertDiagBlocksLowerTriangular" | custom-call | tf_op jit(solution)/shard_map/jit(_solve_triangular)/triangular_solve | solution.py:53
  (80 shorter events, 65.6 us)
Async XLA Ops:
  7.2 79.4 %copy-start = (bf16[3,12,192,192]{3,2,1,0:T(8,128)(2,1)S(1)}, bf16[3,12,192,192]{3,2,1,0:T(8,128)(2,1)}, u32[]{:S(2)}) copy-start(bf16[3,12,192,192]{3,2,1,0:T(8,128)(2,1)} %param.9) | copy-start | bytes 7962628
  7.2 58.4 %copy-start.8 = (f32[2]{0:T(128)S(1)}, f32[2]{0:T(128)}, u32[]{:S(2)}) copy-start(f32[2]{0:T(128)} %param.13) | copy-start | bytes 28
  7.2 61.4 %copy-start.7 = (s32[3,12]{1,0:T(4,128)S(1)}, s32[3,12]{1,0:T(4,128)}, u32[]{:S(2)}) copy-start(s32[3,12]{1,0:T(4,128)} %param.10) | copy-start | bytes 436
  7.2 42.5 %all-gather.4.cloned.1.call-start = ((), (), s32[]{:S(2)}) async-start(), calls=%async_computation | async-start | bytes 2654208 | tf_op jit(solution)/shard_map/all_gather | solution.py:18
  9.2 115.8 %all-gather.6.cloned.1.call-start = ((), (), s32[]{:S(2)}) async-start(), calls=%async_computation.1 | async-start | bytes 2654208 | tf_op jit(solution)/shard_map/all_gather | solution.py:18
  52.8 21.5 %collective-permute-start = (bf16[6,192,256]{2,1,0:T(8,128)(2,1)}, bf16[6,192,256]{2,1,0:T(8,128)(2,1)}, u32[]{:S(2)}, u32[]{:S(2)}) collective-permute-start(bf16[6,192,256]{2,1,0:T(8,128)(2,1)} %gather_fusion), channel_id=1, source_target_pairs={{0,8},{8,16},{16,24},{24,32},{32,40},{40,48},{48,56},{56,64},{64,7... | collective-permute-start | bytes 1769480 | tf_op jit(solution)/shard_map/ppermute | solution.py:10
  59.0 19.3 %collective-permute-start.1 = (bf16[6,192,256]{2,1,0:T(8,128)(2,1)}, bf16[6,192,256]{2,1,0:T(8,128)(2,1)}, u32[]{:S(2)}, u32[]{:S(2)}) collective-permute-start(bf16[6,192,256]{2,1,0:T(8,128)(2,1)} %gather_fusion.1), channel_id=1, source_target_pairs={{0,504},{8,0},{16,8},{24,16},{32,24},{40,32},{48,40},{56,48},{64,5... | collective-permute-start | bytes 1769480 | tf_op jit(solution)/shard_map/ppermute | solution.py:10
  86.6 3.1 copy-start.2
  89.6 0.9 copy-start.4
  90.5 109.9 %all-gather.8.cloned.1.call-start = ((), (), s32[]{:S(2)}) async-start(), calls=%async_computation.2 | async-start | bytes 2654208 | tf_op jit(solution)/shard_map/all_gather | solution.py:18
  128.1 21.5 %collective-permute-start.2 = (bf16[6,192,256]{2,1,0:T(8,128)(2,1)}, bf16[6,192,256]{2,1,0:T(8,128)(2,1)}, u32[]{:S(2)}, u32[]{:S(2)}) collective-permute-start(bf16[6,192,256]{2,1,0:T(8,128)(2,1)} %gather_fusion.3), channel_id=1, source_target_pairs={{0,8},{8,16},{16,24},{24,32},{32,40},{40,48},{48,56},{56,64},{64,7... | collective-permute-start | bytes 1769480 | tf_op jit(solution)/shard_map/ppermute | solution.py:10
  134.3 19.3 %collective-permute-start.3 = (bf16[6,192,256]{2,1,0:T(8,128)(2,1)}, bf16[6,192,256]{2,1,0:T(8,128)(2,1)S(1)}, u32[]{:S(2)}, u32[]{:S(2)}) collective-permute-start(bf16[6,192,256]{2,1,0:T(8,128)(2,1)} %gather_fusion.4), channel_id=1, source_target_pairs={{0,504},{8,0},{16,8},{24,16},{32,24},{40,32},{48,40},{56,48},{64,5... | collective-permute-start | bytes 1769480 | tf_op jit(solution)/shard_map/ppermute | solution.py:10
  161.8 3.1 copy-start.3
  161.8 3.1 copy-start.5
  166.0 336.1 %all-reduce.6.cloned.1.call-start = ((), (), s32[]{:S(2)}) async-start(), calls=%async_computation.3 | async-start | bytes 1048576 | tf_op jit(solution)/shard_map/psum | solution.py:49
  203.5 21.5 %collective-permute-start.4 = (bf16[6,192,256]{2,1,0:T(8,128)(2,1)}, bf16[6,192,256]{2,1,0:T(8,128)(2,1)}, u32[]{:S(2)}, u32[]{:S(2)}) collective-permute-start(bf16[6,192,256]{2,1,0:T(8,128)(2,1)} %gather_fusion.6), channel_id=1, source_target_pairs={{0,8},{8,16},{16,24},{24,32},{32,40},{40,48},{48,56},{56,64},{64,7... | collective-permute-start | bytes 1769480 | tf_op jit(solution)/shard_map/ppermute | solution.py:10
  209.7 19.3 %collective-permute-start.5 = (bf16[6,192,256]{2,1,0:T(8,128)(2,1)}, bf16[6,192,256]{2,1,0:T(8,128)(2,1)S(1)}, u32[]{:S(2)}, u32[]{:S(2)}) collective-permute-start(bf16[6,192,256]{2,1,0:T(8,128)(2,1)} %gather_fusion.7), channel_id=1, source_target_pairs={{0,504},{8,0},{16,8},{24,16},{32,24},{40,32},{48,40},{56,48},{64,5... | collective-permute-start | bytes 1769480 | tf_op jit(solution)/shard_map/ppermute | solution.py:10
  237.2 3.0 copy-start.1
  242.2 341.7 %all-reduce.8.cloned.1.call-start = ((), (), s32[]{:S(2)}) async-start(), calls=%async_computation.4 | async-start | bytes 1048576 | tf_op jit(solution)/shard_map/psum | solution.py:49
  588.6 0.7 copy-start.6
Sparse Core Ops, SparseCore 0:
  10.7 38.9 all-gather.3
  90.6 34.3 all-gather.5
  166.1 34.2 all-gather.7
  242.3 259.7 all-reduce.5
  504.4 79.4 all-reduce.7
